TPU v7x, 256 devices: a whole 4x4x8 slice. The times are simulated.
256 devices in a mesh: expert: 64 (over y, z, core), hidden: 4 (over x).
Axes of the slice: x: 4, y: 4, z: 8, core: 2. Of those that a mesh axis runs over, the one named last changes fastest.
Arguments:
- tokens: bfloat16 [8192, 4096], P('expert', 'hidden'), may hold values from -6 to 6
- routes: int32 [8192, 8], P('expert'), may hold values from 0 to 63, all different within a row; in each aligned block of 128 rows (0 to 127, 128 to 255, ...) at most 24 rows name the same one
- route_gates: float32 [8192, 8], P('expert'), may hold values from 0.03 to 0.3
- loss_weights: float32 [8192], P('expert'), may hold values from 0.25 to 4
- damping: float32 [1], replicated, may hold values from 1 to 16
- w_gate: bfloat16 [64, 4096, 768], P('expert', None, 'hidden'), may hold values from -0.09375 to 0.09375
- w_up: bfloat16 [64, 4096, 768], P('expert', None, 'hidden'), may hold values from -0.09375 to 0.09375
- direction: bfloat16 [64, 768, 4096], P('expert', 'hidden'), may hold values from -6 to 6
- residual: bfloat16 [64, 768, 4096], P('expert', 'hidden'), may hold values from -6 to 6
Outputs:
- solution_step: bfloat16 [64, 768, 4096], P('expert', 'hidden')
- new_residual: bfloat16 [64, 768, 4096], P('expert', 'hidden')
- new_direction: bfloat16 [64, 768, 4096], P('expert', 'hidden')
Inputs may be any that keep to these rules, and one draw needn't show every extreme that they name: `routes`: each token names 8 different experts. Among the tokens of one index of expert (aligned blocks of 128 rows) no expert is named more than 24 times, and in every draw some block names some expert exactly 24 times.
All inputs are finite; a program needn't handle non-finite values.
Results may differ from a plain program's by a relative error of at most 0.011.
Values may be sent and summed in bfloat16 or wider, within the bound.
A program may use at most 128 MiB of HBM per device.

v0:
```python
import jax
import jax.numpy as jnp
from jax import lax
from jax.sharding import PartitionSpec as P


def per_device(
    tokens, routes, route_gates, loss_weights, damping, w_gate, w_up, direction, residual
):
    experts = lax.axis_size("expert")
    tok_rows, top_routes = routes.shape
    capacity = min(tok_rows, 3 * tok_rows * top_routes // (2 * experts))
    route_count = tok_rows * top_routes
    slot_count = experts * capacity
    flat_routes = routes.reshape(-1)
    one_hot = (flat_routes[:, None] == jnp.arange(experts, dtype=jnp.int32)[None, :]).astype(
        jnp.int32
    )
    earlier = jnp.cumsum(one_hot, axis=0) - one_hot
    position = jnp.sum(earlier * one_hot, axis=1)
    slot_of_route = flat_routes * capacity + position
    route_of_slot = (
        jnp.full((slot_count,), route_count, jnp.int32)
        .at[slot_of_route]
        .set(jnp.arange(route_count, dtype=jnp.int32))
    )
    filled = route_of_slot < route_count
    safe_route = jnp.minimum(route_of_slot, route_count - 1)
    token_of_slot = safe_route // top_routes

    def pack_rows(source_rows, index):
        picked = source_rows[index]
        return jnp.where(filled[:, None], picked, jnp.zeros((), picked.dtype)).reshape(
            experts, capacity, -1
        )

    gate_local = w_gate[0]
    up_local = w_up[0]
    whole_tokens = lax.all_gather(tokens, "hidden", axis=1, tiled=True)
    send_rows = pack_rows(whole_tokens, token_of_slot)
    arrived = lax.all_to_all(send_rows, "expert", split_axis=0, concat_axis=0, tiled=True).reshape(
        slot_count, -1
    )
    pre_gate = jnp.dot(arrived, gate_local, preferred_element_type=jnp.float32)
    pre_up = jnp.dot(arrived, up_local, preferred_element_type=jnp.float32)
    hidden = (jax.nn.silu(pre_gate) * pre_up).astype(jnp.bfloat16)
    hidden_full = lax.all_gather(hidden, "hidden", axis=1, tiled=True)
    search_cols = lax.all_to_all(direction[0], "hidden", split_axis=1, concat_axis=0, tiled=True)
    tangent = jnp.dot(hidden_full, search_cols, preferred_element_type=jnp.float32).astype(
        jnp.bfloat16
    )
    returned = lax.all_to_all(
        tangent.reshape(experts, capacity, -1), "expert", split_axis=0, concat_axis=0, tiled=True
    ).reshape(slot_count, -1)
    per_route = returned[slot_of_route].reshape(tok_rows, top_routes, -1)
    combined = jnp.einsum("tjd,tj->td", per_route.astype(jnp.float32), route_gates)
    scaled = combined * loss_weights[:, None]
    cotangent = (
        (route_gates[:, :, None] * scaled[:, None, :]).astype(jnp.bfloat16).reshape(route_count, -1)
    )
    send_back = pack_rows(cotangent, safe_route)
    back_rows = lax.all_to_all(
        send_back, "expert", split_axis=0, concat_axis=0, tiled=True
    ).reshape(slot_count, -1)
    curvature_cols = lax.dot_general(
        hidden_full, back_rows, (((0,), (0,)), ((), ())), preferred_element_type=jnp.float32
    )
    curvature = lax.all_to_all(curvature_cols, "hidden", split_axis=0, concat_axis=1, tiled=True)
    search = direction[0].astype(jnp.float32)
    resid = residual[0].astype(jnp.float32)
    image = search + curvature / damping[0]
    pq_total, rr_total = lax.psum(
        (jnp.sum(search * image), jnp.sum(resid * resid)), ("expert", "hidden")
    )
    alpha_step = rr_total / pq_total
    updated = resid - alpha_step * image
    rr_new = lax.psum(jnp.sum(updated * updated), ("expert", "hidden"))
    beta_ratio = rr_new / rr_total
    solution_step = (alpha_step * search).astype(jnp.bfloat16)[None]
    new_residual = updated.astype(jnp.bfloat16)[None]
    new_direction = (updated + beta_ratio * search).astype(jnp.bfloat16)[None]
    return (solution_step, new_residual, new_direction)


def solution(mesh):
    return jax.shard_map(
        per_device,
        mesh=mesh,
        in_specs=(
            P("expert", "hidden"),
            P("expert", None),
            P("expert", None),
            P("expert"),
            P(),
            P("expert", None, "hidden"),
            P("expert", None, "hidden"),
            P("expert", "hidden", None),
            P("expert", "hidden", None),
        ),
        out_specs=(
            P("expert", "hidden", None),
            P("expert", "hidden", None),
            P("expert", "hidden", None),
        ),
        check_vma=False,
    )
```

profile of v0, /device:TPU:1, one launch (start us, length us, event | category | flops | bytes accessed | tf_op | source)
XLA Modules:
  0.0 834.8 jit_solution(10602769745563700831)
XLA Ops:
  7.2 0.0 copy-start
  7.2 0.0 all-gather.3.cloned.1.call-start
  7.2 0.7 all-gather.3.cloned.1.call-update
  7.9 0.0 all-gather.5.cloned.1.call-start
  8.0 0.8 copy.30
  8.8 0.1 eq.29
  8.8 0.1 eq.25
  9.0 18.0 %reduce-window.6 = s32[64,8,128]{2,1,0:T(8,128)S(1)} reduce-window(s32[64,8,128]{2,1,0:T(8,128)S(1)} %fusion.25, s32[]{:T(128)} %constant.30.clone.1), window={size=1x1x128 pad=0_0x0_0x127_0}, to_apply=%region_2.3 | reduce-window | flops 8323072 | bytes 524292 | tf_op jit(solution)/shard_map/reduce-window
  27.0 0.1 slice.14
  27.1 0.1 copy.32
  27.3 0.1 copy.33
  27.4 0.7 broadcast_multiply_fusion
  28.1 0.1 copy.29
  28.2 0.1 mul.88
  28.3 0.1 broadcast_add_fusion
  28.4 0.1 fusion.24
  28.5 4.3 scatter_custom_fusion
  32.9 0.1 broadcast_in_dim.43
  33.0 5.2 all-gather.3.cloned.1.call-done
  38.2 23.4 %gather_fusion = bf16[1536,4096]{1,0:T(8,128)(2,1)} fusion(bf16[128,4096]{1,0:T(8,128)(2,1)} %all-gather.3.cloned.1.call-done, s32[2048]{0:T(1024)S(1)} %pad_clamp_fusion.1), kind=kCustom, calls=%fused_computation | custom fusion | bytes 25171968 | tf_op jit(solution)/shard_map/gather | solution.py:32
  61.6 6.3 broadcast_select_fusion
  67.9 288.5 %all_to_all.44 = bf16[64,24,4096]{2,1,0:T(8,128)(2,1)S(1)} all-to-all(bf16[64,24,4096]{2,1,0:T(8,128)(2,1)S(1)} %broadcast_select_fusion), channel_id=1, replica_groups=mesh['expert'=64,'hidden'=4] {'expert'}, dimensions={0} | all-to-all | bytes 25165824 | tf_op jit(solution)/shard_map/all_to_all | solution.py:41
  356.4 0.0 copy-done
  356.4 4.3 fusion.17
  360.7 0.0 copy-done.8
  360.7 0.0 copy-start.3
  360.7 5.2 fusion.13
  365.9 0.0 all-gather.5.cloned.1.call-update
  365.9 0.0 copy-done.3
  365.9 2.4 all_to_all.32
  368.3 1.9 copy.35
  370.2 39.1 %all_to_all.45 = bf16[192,4,1024]{2,0,1:T(8,128)(2,1)} all-to-all(bf16[192,4,1024]{2,0,1:T(8,128)(2,1)S(1)} %copy.35), channel_id=1, replica_groups=mesh['expert'=64,'hidden'=4] {'hidden'}, dimensions={1} | all-to-all | bytes 3145728 | tf_op jit(solution)/shard_map/all_to_all | solution.py:48
  409.3 4.1 all-gather.5.cloned.1.call-done
  413.4 6.5 convolution_convert_fusion
  419.9 6.0 all-to-all-start.2
  426.0 0.0 copy-done.5
  426.0 0.1 copy.34
  426.1 0.1 copy.38
  426.2 0.1 mul.92
  426.4 73.0 %all-to-all-done.2 = bf16[64,24,1024]{2,1,0:T(8,128)(2,1)} async-done(((bf16[64,24,1024]{2,1,0:T(8,128)(2,1)}), bf16[64,24,1024]{2,1,0:T(8,128)(2,1)}, u32[]{:S(2)}, u32[]{:S(2)}) %all-to-all-start.2) | async-done | bytes 3145760 | tf_op jit(solution)/shard_map/all_to_all | solution.py:52
  499.4 8.4 %gather_fusion.1 = bf16[1024,1024]{1,0:T(8,128)(2,1)} fusion(bf16[1536,1024]{1,0:T(8,128)(2,1)} %bitcast.15, s32[1024]{0:T(1024)S(1)} %broadcast_clamp_fusion), kind=kCustom, calls=%fused_computation.1 | custom fusion | bytes 4198400 | tf_op jit(solution)/shard_map/gather | solution.py:55
  507.7 2.3 fusion.14
  510.0 0.0 copy-done.6
  510.0 0.2 bitcast_multiply_fusion.1
  510.2 1.7 fusion
  511.9 9.7 %gather_fusion.2 = bf16[1536,1024]{1,0:T(8,128)(2,1)} fusion(bf16[1024,1024]{1,0:T(8,128)(2,1)} %fusion, s32[2048]{0:T(1024)S(1)} %pad_clamp_fusion), kind=kCustom, calls=%fused_computation.2 | custom fusion | bytes 6297600 | tf_op jit(solution)/shard_map/gather | solution.py:32
  521.5 2.1 broadcast_select_fusion.1
  523.6 0.0 copy-start.7
  523.6 79.1 %all_to_all.46 = bf16[64,24,1024]{2,1,0:T(8,128)(2,1)S(1)} all-to-all(bf16[64,24,1024]{2,1,0:T(8,128)(2,1)S(1)} %broadcast_select_fusion.1), channel_id=1, replica_groups=mesh['expert'=64,'hidden'=4] {'expert'}, dimensions={0} | all-to-all | bytes 6291456 | tf_op jit(solution)/shard_map/all_to_all | solution.py:62
  602.8 4.3 fusion.30
  607.0 4.6 all-to-all-start.4
  612.3 37.1 %all-to-all-done.4 = f32[4,192,1024]{2,1,0:T(8,128)} async-done(((f32[4,192,1024]{2,1,0:T(8,128)}), f32[4,192,1024]{2,1,0:T(8,128)}, u32[]{:S(2)}, u32[]{:S(2)}) %all-to-all-start.4) | async-done | bytes 3145760 | tf_op jit(solution)/shard_map/all_to_all | solution.py:68
  649.4 4.6 fusion.21
  654.0 0.4 copy.40
  654.4 0.0 copy-start.2
  654.4 1.2 copy-done.4
  655.6 1.6 fusion.5
  657.2 74.2 %all-reduce = (f32[]{:T(128)}, f32[]{:T(128)}) all-reduce(f32[]{:T(128)} %get-tuple-element.12, f32[]{:T(128)} %get-tuple-element.13), channel_id=1, replica_groups=mesh['expert'=64,'hidden'=4] {'expert','hidden'}, use_global_device_ids=true, to_apply=%region_1.2 | all-reduce | flops 2 | bytes 16 | tf_op jit(solution)/shard_map/psum | solution.py:72
  732.7 3.3 fusion.7
  736.0 74.3 %psum.23 = f32[]{:T(128)} all-reduce(f32[]{:T(128)} %fusion.7), channel_id=1, replica_groups=mesh['expert'=64,'hidden'=4] {'expert','hidden'}, use_global_device_ids=true, to_apply=%region_9.10 | all-reduce | flops 1 | bytes 8 | tf_op jit(solution)/shard_map/psum | solution.py:77
  811.6 5.6 copy.36
  817.3 5.4 div.56
  822.6 5.3 fusion.12
  827.9 0.0 copy-done.1
  (17 shorter events, 0.1 us)
Async XLA Ops:
  7.2 349.3 %copy-start = (bf16[1,4096,192]{1,2,0:T(8,128)(2,1)S(1)}, bf16[1,4096,192]{1,2,0:T(8,128)(2,1)}, u32[]{:S(2)}) copy-start(bf16[1,4096,192]{1,2,0:T(8,128)(2,1)} %param.14) | copy-start | bytes 4718596
  7.2 31.0 %all-gather.3.cloned.1.call-start = ((), (), s32[]{:S(2)}) async-start(), calls=%async_computation.5 | async-start | bytes 1310720 | tf_op jit(solution)/shard_map/all_gather | solution.py:39
  7.9 405.5 %all-gather.5.cloned.1.call-start = ((), (), s32[]{:S(2)}) async-start(), calls=%async_computation.6 | async-start | bytes 2949120 | tf_op jit(solution)/shard_map/all_gather | solution.py:47
  356.4 4.3 copy-start.8
  360.7 5.2 copy-start.3
  419.9 6.1 copy-start.5
  419.9 79.4 %all-to-all-start.2 = ((bf16[64,24,1024]{2,1,0:T(8,128)(2,1)}), bf16[64,24,1024]{2,1,0:T(8,128)(2,1)}, u32[]{:S(2)}, u32[]{:S(2)}) async-start(bf16[64,24,1024]{2,1,0:T(8,128)(2,1)} %bitcast.94), calls=%async_computation.2 | async-start | bytes 6291456 | tf_op jit(solution)/shard_map/all_to_all | solution.py:52
  499.4 10.6 %copy-start.6 = (f32[128]{0:T(128)S(1)}, f32[128]{0:T(128)}, u32[]{:S(2)}) copy-start(f32[128]{0:T(128)} %param.12) | copy-start | bytes 1540
  523.6 79.2 %copy-start.7 = (bf16[1536,768]{0,1:T(8,128)(2,1)S(1)}, bf16[1536,768]{0,1:T(8,128)(2,1)}, u32[]{:S(2)}) copy-start(bf16[1536,768]{0,1:T(8,128)(2,1)} %all-gather.5.cloned.1.call-done) | copy-start | bytes 7077892
  607.0 42.4 %all-to-all-start.4 = ((f32[4,192,1024]{2,1,0:T(8,128)}), f32[4,192,1024]{2,1,0:T(8,128)}, u32[]{:S(2)}, u32[]{:S(2)}) async-start(f32[4,192,1024]{2,1,0:T(8,128)} %fusion.30), calls=%async_computation.4 | async-start | bytes 6291456 | tf_op jit(solution)/shard_map/all_to_all | solution.py:68
  654.0 1.6 copy-start.4
  654.4 2.7 copy-start.2
  817.3 10.7 %copy-start.1 = (bf16[1,4096,192]{1,2,0:T(8,128)(2,1)S(1)}, bf16[1,4096,192]{1,2,0:T(8,128)(2,1)}, u32[]{:S(2)}) copy-start(bf16[1,4096,192]{1,2,0:T(8,128)(2,1)} %param.14) | copy-start | bytes 4718596
Sparse Core Ops, SparseCore 0:
  9.8 28.3 all-gather.2
  366.1 47.3 all-gather.4
where the time goes:
time: 836 us; the launch traced here: 835 us
  blocking collectives  555 us (66%)
  waiting for transfers between devices  120 us (14%)
  local copies, waits for them, and re-layouts  64.5 us (8%)
  other arithmetic  44 us (5%)
  matrix products  22.5 us (3%)
  between operations  17.6 us (2%)
  starting transfers between devices  10.8 us (1%)
    all_to_all x1, blocking collectives, per_device(): lax.all_to_all(send_rows, 'expert', split_axis=0, concat_axis=0, tiled=True)  289 us
    all_to_all x1, blocking collectives, per_device(): lax.all_to_all(send_back, 'expert', split_axis=0, concat_axis=0, tiled=True)  79.1 us
    psum x1, blocking collectives, per_device(): rr_new = lax.psum(jnp.sum(updated * updated), ('expert', 'hidden'))  74.3 us
    psum x1, blocking collectives, per_device(): lax.psum((jnp.sum(search * image), jnp.sum(resid * resid)), ('expert', 'h...  74.2 us
    all_to_all x1, waiting for transfers between devices, per_device(): lax.all_to_all(tangent.reshape(experts, capacity, -1), 'expert', split_ax...  73 us
    all_to_all x1, blocking collectives, per_device(): lax.all_to_all(direction[0], 'hidden', split_axis=1, concat_axis=0, tiled...  39.1 us
    all_to_all x1, waiting for transfers between devices, per_device(): lax.all_to_all(curvature_cols, 'hidden', split_axis=0, concat_axis=1, til...  37.1 us
    gather x2, local copies, waits for them, and re-layouts, pack_rows(): picked = source_rows[index]  33 us
  transfers between devices with their start and end apart: 4, of which 4 were waited for; matrix products, arithmetic and copies ran while one was open for 3% of the time, Pallas kernels for 0%

commit v1 on v0

v1 whole, which is shorter than its diff:
```python
import jax
import jax.numpy as jnp
from jax import lax
from jax.experimental import pallas as pl
from jax.experimental.pallas import tpu as pltpu
from jax.sharding import PartitionSpec as P

MESH = pl.DeviceIdType.MESH
BF = jnp.bfloat16
F32 = jnp.float32
NY, NZ, NC, NX = 4, 8, 2, 4
NQ = NY * NC
CAP = 24
TOK = 128
CH = 256
NK = 4
VMEM = pl.BlockSpec(memory_space=pltpu.VMEM)
ANY = pl.BlockSpec(memory_space=pl.ANY)


class Place:
    def __init__(self):
        self.e = lax.axis_index("expert")
        self.x = lax.axis_index("hidden")
        self.y = self.e // (NZ * NC)
        self.z = (self.e // NC) % NZ
        self.c = self.e % NC

    def expert(self, dy, dz, dc):
        return (
            ((self.y + dy) % NY) * (NZ * NC)
            + ((self.z + dz) % NZ) * NC
            + (self.c + dc) % NC
        )

    def q(self, q):
        return (self.expert(q // NC, 0, q % NC), self.x)

    def dz(self, d):
        return (self.expert(0, d, 0), self.x)

    def dx(self, d):
        return (self.e, self.xi(d))

    def xi(self, d):
        return (self.x + d) % NX


def inverse(q):
    return ((NY - q // NC) % NY) * NC + q % NC


def enter(peers):
    barrier = pltpu.get_barrier_semaphore()
    for peer in peers:
        pl.semaphore_signal(barrier, inc=1, device_id=peer, device_id_type=MESH)
    pl.semaphore_wait(barrier, len(peers))


def send(src, dst, ssem, rsem, peer):
    pltpu.make_async_remote_copy(
        src_ref=src, dst_ref=dst, send_sem=ssem, recv_sem=rsem, device_id=peer, device_id_type=MESH
    ).start()


def wait_bytes(ref, sem):
    pltpu.make_async_copy(ref, ref, sem).wait()


def pair_blocks(pi):
    return (0, 4) if pi == 3 else (pi + 1, NZ - 1 - pi)


def slot_matrix(tab_ref, pi, weighted):
    r0, r1 = pair_blocks(pi)
    slot = lax.broadcasted_iota(jnp.int32, (CAP, TOK), 0).astype(F32)
    zero = jnp.zeros((CAP, TOK), F32)
    rows = []
    for q in range(NQ):
        parts = []
        for r in (r0, r1):
            hit = tab_ref[r, q : q + 1, :] == slot
            value = tab_ref[r, NQ + q : NQ + q + 1, :] if weighted else jnp.ones((1, TOK), F32)
            parts.append(jnp.where(hit, value, 0.0))
        rows.append(jnp.concatenate([parts[0], zero], axis=1))
        rows.append(jnp.concatenate([zero, parts[1]], axis=1))
    return jnp.concatenate(rows, axis=0)


def lanes(k):
    return pl.ds(k * CH, CH)


def sign(k):
    return 1 if k % 2 == 0 else -1


def rel(r):
    return r % NZ


def tokens_kernel(
    routes_ref, gates_ref, tok_ref, wg_ref, wu_ref, dir_ref,
    x_ref, w_ref, dirc_ref, tab_ref,
    own_tab, slots, zb, ysend, wgv, wuv, wsend, wrecv,
    tab_ssem, tab_rsem, z_ssem, z_rsem, y_ssem, y_rsem, d_ssem, d_rsem, w_ssem, w_rsem, loc,
):
    at = Place()
    wg_load = pltpu.make_async_copy(wg_ref, wgv, loc.at[0])
    wu_load = pltpu.make_async_copy(wu_ref, wuv, loc.at[1])
    wg_load.start()
    wu_load.start()
    depth = dir_ref.shape[1] // NX
    ff = dir_ref.shape[0]
    own_dir = pltpu.make_async_copy(
        dir_ref.at[:, pl.ds(pl.multiple_of(at.x * depth, depth), depth)], dirc_ref.at[at.x], loc.at[2]
    )
    own_dir.start()

    row = lax.broadcasted_iota(jnp.int32, (NZ * NQ, TOK), 0)
    ids = (
        ((at.y + ((row >> 1) & 3)) & (NY - 1)) * (NZ * NC)
        + ((at.z + (row >> 3)) & (NZ - 1)) * NC
        + ((at.c + row) & 1)
    )
    named = jnp.zeros((NZ * NQ, TOK), F32)
    gate = jnp.zeros((NZ * NQ, TOK), F32)
    for j in range(routes_ref.shape[0]):
        same = routes_ref[j : j + 1, :] == ids
        named = named + jnp.where(same, 1.0, 0.0)
        gate = gate + jnp.where(same, gates_ref[j : j + 1, :], 0.0)
    before = (
        lax.broadcasted_iota(jnp.int32, (TOK, TOK), 0) < lax.broadcasted_iota(jnp.int32, (TOK, TOK), 1)
    )
    place = jnp.dot(
        named.astype(BF), jnp.where(before, 1.0, 0.0).astype(BF), preferred_element_type=F32
    )
    place = jnp.where(named > 0.0, place, -1.0)
    for r in range(NZ):
        own_tab[r, 0:NQ, :] = place[r * NQ : (r + 1) * NQ]
        own_tab[r, NQ : 2 * NQ, :] = gate[r * NQ : (r + 1) * NQ]
    tab_ref[0] = own_tab[0]

    enter(
        [at.q(q) for q in range(1, NQ)] + [at.dz(d) for d in range(1, NZ)] + [at.dx(d) for d in range(1, NX)]
    )
    for r in (1, 7, 2, 6, 3, 5, 4):
        send(own_tab.at[r], tab_ref.at[rel(-r)], tab_ssem, tab_rsem.at[rel(-r)], at.dz(r))
    for k in range(NK):
        for d in (1, -1):
            send(
                tok_ref.at[:, lanes(k)], zb.at[k, rel(-d)], z_ssem, z_rsem.at[k, rel(-d)], at.dz(d)
            )
    for d in (2, 1, 3):
        send(
            dir_ref.at[:, pl.ds(pl.multiple_of(at.xi(d) * depth, depth), depth)],
            dirc_ref.at[at.x], d_ssem, d_rsem, at.dx(d),
        )

    wg_load.wait()
    wu_load.wait()
    step = 64
    for d in (2, 1, 3, 0):
        base = at.xi(d) * depth

        def join(i, _, d=d, base=base):
            rows = pl.ds(pl.multiple_of(base + i * step, step), step)
            both = jnp.concatenate([wgv[rows, :], wuv[rows, :]], axis=1)
            out_rows = pl.ds(pl.multiple_of(i * step, step), step)
            if d == 0:
                wrecv[at.x, out_rows, :] = both
            else:
                wsend[d, out_rows, :] = both
            return 0

        lax.fori_loop(0, depth // step, join, 0)
        if d:
            send(wsend.at[d], wrecv.at[at.x], w_ssem, w_rsem, at.dx(d))

    for s in range(1, 5):
        pi = s - 1
        for r in pair_blocks(pi):
            if r:
                wait_bytes(tab_ref.at[r], tab_rsem.at[r])
        slots[pi] = slot_matrix(tab_ref, pi, False).astype(BF)
        for k in range(NK):
            d = sign(k)
            wait_bytes(zb.at[k, rel(-d * s)], z_rsem.at[k, rel(-d * s)])
            if s < 4:
                wait_bytes(zb.at[k, rel(d * s)], z_rsem.at[k, rel(d * s)])
                send(
                    zb.at[k, rel(-d * s)], zb.at[k, rel(-d * (s + 1))],
                    z_ssem, z_rsem.at[k, rel(-d * (s + 1))], at.dz(d),
                )
            if s < 3:
                send(
                    zb.at[k, rel(d * s)], zb.at[k, rel(d * (s + 1))],
                    z_ssem, z_rsem.at[k, rel(d * (s + 1))], at.dz(-d),
                )
            r0, r1 = pair_blocks(pi)
            first = tok_ref[:, lanes(k)] if r0 == 0 else zb[k, r0]
            block = jnp.concatenate([first, zb[k, r1]], axis=0)
            picked = jnp.dot(slots[pi], block, preferred_element_type=F32).astype(BF)
            rows = pl.ds(pi * 2 * CAP, 2 * CAP)
            x_ref[0, rows, lanes(k)] = picked[0 : 2 * CAP]
            for q in range(1, NQ):
                ysend[q, rows, lanes(k)] = picked[q * 2 * CAP : (q + 1) * 2 * CAP]
            for q in range(1, NQ):
                send(
                    ysend.at[q, rows, lanes(k)], x_ref.at[inverse(q), rows, lanes(k)],
                    y_ssem, y_rsem, at.q(q),
                )

    own_dir.wait()
    wait_bytes(wsend.at[pl.ds(1, 3)], w_rsem)

    def split(i, _):
        rows = pl.ds(pl.multiple_of(i * step, step), step)
        parts = [wrecv[j, rows, :] for j in range(NX)]
        w_ref[rows, :] = jnp.concatenate(
            [p[:, :ff] for p in parts] + [p[:, ff:] for p in parts], axis=1
        )
        return 0

    lax.fori_loop(0, depth // step, split, 0)
    wait_bytes(dirc_ref.at[pl.ds(1, 3)], d_rsem)
    wait_bytes(x_ref.at[pl.ds(1, NQ - 1)], y_rsem)
    wait_bytes(own_tab.at[pl.ds(1, NZ - 1)], tab_ssem)
    wait_bytes(zb.at[:, pl.ds(1, NZ - 1)], z_ssem)
    wait_bytes(x_ref.at[pl.ds(1, NQ - 1)], y_ssem)
    wait_bytes(dirc_ref.at[pl.ds(1, 3)], d_ssem)
    wait_bytes(wsend.at[pl.ds(1, 3)], w_ssem)


def hidden_kernel(
    p_ref, h_ref, far, acc, accin, near,
    f_ssem, f_rsem, a_ssem, a_rsem, n_ssem, n_rsem, h_ssem, h_rsem,
):
    at = Place()
    subs = far.shape[0]
    rows_of = far.shape[1]
    ff = h_ref.shape[2]
    step = 16
    enter([at.dx(1), at.dx(-1)])

    def rows(u):
        return pl.ds(u * rows_of, rows_of)

    for u in range(subs):
        d = sign(u)
        send(p_ref.at[at.xi(2), rows(u)], far.at[u], f_ssem, f_rsem.at[u], at.dx(-d))
        send(p_ref.at[at.xi(d), rows(u)], near.at[u], n_ssem, n_rsem.at[u], at.dx(d))
    for u in range(subs):
        d = sign(u)
        wait_bytes(far.at[u], f_rsem.at[u])

        def add(i, _, u=u, d=d):
            sub = pl.ds(pl.multiple_of(i * step, step), step)
            mine = p_ref[at.xi(-d), pl.ds(pl.multiple_of(u * rows_of + i * step, step), step), :]
            acc[u, sub, :] = (far[u, sub, :].astype(F32) + mine.astype(F32)).astype(BF)
            return 0

        lax.fori_loop(0, rows_of // step, add, 0)
        send(acc.at[u], accin.at[u], a_ssem, a_rsem.at[u], at.dx(-d))
    for u in range(subs):
        d = sign(u)
        wait_bytes(near.at[u], n_rsem.at[u])
        wait_bytes(accin.at[u], a_rsem.at[u])

        def act(i, _, u=u):
            sub = pl.ds(pl.multiple_of(i * step, step), step)
            whole = pl.ds(pl.multiple_of(u * rows_of + i * step, step), step)

            def total(cols):
                return (
                    p_ref[at.x, whole, cols].astype(F32)
                    + accin[u, sub, cols].astype(F32)
                    + near[u, sub, cols].astype(F32)
                )

            v = total(pl.ds(0, ff))
            h_ref[at.x, whole, :] = (v / (1.0 + jnp.exp(-v)) * total(pl.ds(ff, ff))).astype(BF)
            return 0

        lax.fori_loop(0, rows_of // step, act, 0)
        for t in (d, -d):
            send(
                h_ref.at[at.x, rows(u)], h_ref.at[at.x, rows(u)],
                h_ssem, h_rsem.at[u, 0 if t == d else 1], at.dx(t),
            )
    for u in range(subs):
        d = sign(u)
        wait_bytes(h_ref.at[at.xi(-d), rows(u)], h_rsem.at[u, 0])
        send(
            h_ref.at[at.xi(-d), rows(u)], h_ref.at[at.xi(-d), rows(u)],
            h_ssem, h_rsem.at[u, 2], at.dx(d),
        )
    for u in range(subs):
        d = sign(u)
        wait_bytes(h_ref.at[at.xi(d), rows(u)], h_rsem.at[u, 1])
        wait_bytes(h_ref.at[at.xi(2), rows(u)], h_rsem.at[u, 2])
    wait_bytes(far, f_ssem)
    wait_bytes(near, n_ssem)
    wait_bytes(acc, a_ssem)
    wait_bytes(h_ref.at[pl.ds(0, 3)], h_ssem)


def cotangent_kernel(
    tan_ref, tab_ref, lw_ref, cot_ref,
    back, fwd, recv, own, asend, arecv, bsend, brecv, zb, ysend,
    t_ssem, t_rsem, a_ssem, a_rsem, b_ssem, b_rsem, z_ssem, z_rsem, y_ssem, y_rsem,
):
    at = Place()

    def rows(pi):
        return pl.ds(pi * 2 * CAP, 2 * CAP)

    enter([at.q(q) for q in range(1, NQ)] + [at.dz(1), at.dz(-1)])
    for t in range(NK + 3):
        for k in range(NK):
            if 0 <= t - k < 4:
                pi = 3 - (t - k)
                for q in range(1, NQ):
                    send(
                        tan_ref.at[q, rows(pi), lanes(k)], recv.at[inverse(q), rows(pi), lanes(k)],
                        t_ssem, t_rsem.at[k, pi], at.q(q),
                    )
    for pi in (3, 2, 1, 0):
        both = slot_matrix(tab_ref, pi, True)
        fwd[pi] = both.astype(BF)
        back[pi] = both.T.astype(BF)

    def partial(k, pi):
        wait_bytes(recv.at[pl.ds(1, NQ - 1), rows(pi), lanes(k)], t_rsem.at[k, pi])
        arrived = jnp.concatenate(
            [tan_ref[0, rows(pi), lanes(k)]] + [recv[q, rows(pi), lanes(k)] for q in range(1, NQ)],
            axis=0,
        )
        return jnp.dot(back[pi], arrived, preferred_element_type=F32)

    def stage(k, n):
        d = sign(k)
        if n < 4:
            pi = 3 - n
            both = partial(k, pi)
            low, high = both[:TOK], both[TOK:]
            if n == 0:
                own[k] = low
                asend[k, 0] = high.astype(BF)
            else:
                s = 4 - n
                ahead, behind = (low, high) if d == 1 else (high, low)
                wait_bytes(arecv.at[k, n - 1], a_rsem.at[k, n - 1])
                asend[k, n] = (arecv[k, n - 1].astype(F32) + ahead).astype(BF)
                if n == 1:
                    bsend[k, 0] = behind.astype(BF)
                else:
                    wait_bytes(brecv.at[k, n - 2], b_rsem.at[k, n - 2])
                    bsend[k, n - 1] = (brecv[k, n - 2].astype(F32) + behind).astype(BF)
                send(bsend.at[k, n - 1], brecv.at[k, n - 1], b_ssem, b_rsem.at[k, n - 1], at.dz(-d))
            send(asend.at[k, n], arecv.at[k, n], a_ssem, a_rsem.at[k, n], at.dz(d))
            return
        if n == 4:
            wait_bytes(arecv.at[k, 3], a_rsem.at[k, 3])
            wait_bytes(brecv.at[k, 2], b_rsem.at[k, 2])
            combined = own[k] + arecv[k, 3].astype(F32) + brecv[k, 2].astype(F32)
            zb[k, 0] = (combined * lw_ref[...]).astype(BF)
            for t in (d, -d):
                send(zb.at[k, 0], zb.at[k, rel(-t)], z_ssem, z_rsem.at[k, rel(-t)], at.dz(t))
            return
        s = n - 4
        pi = s - 1
        wait_bytes(zb.at[k, rel(-d * s)], z_rsem.at[k, rel(-d * s)])
        if s < 4:
            wait_bytes(zb.at[k, rel(d * s)], z_rsem.at[k, rel(d * s)])
            send(
                zb.at[k, rel(-d * s)], zb.at[k, rel(-d * (s + 1))],
                z_ssem, z_rsem.at[k, rel(-d * (s + 1))], at.dz(d),
            )
        if s < 3:
            send(
                zb.at[k, rel(d * s)], zb.at[k, rel(d * (s + 1))],
                z_ssem, z_rsem.at[k, rel(d * (s + 1))], at.dz(-d),
            )
        r0, r1 = pair_blocks(pi)
        block = jnp.concatenate([zb[k, r0], zb[k, r1]], axis=0)
        picked = jnp.dot(fwd[pi], block, preferred_element_type=F32).astype(BF)
        cot_ref[0, rows(pi), lanes(k)] = picked[0 : 2 * CAP]
        for q in range(1, NQ):
            ysend[q, rows(pi), lanes(k)] = picked[q * 2 * CAP : (q + 1) * 2 * CAP]
        for q in range(1, NQ):
            send(
                ysend.at[q, rows(pi), lanes(k)], cot_ref.at[inverse(q), rows(pi), lanes(k)],
                y_ssem, y_rsem, at.q(q),
            )

    for t in range(NK + 8):
        for k in range(NK):
            if 0 <= t - k < 9:
                stage(k, t - k)

    wait_bytes(cot_ref.at[pl.ds(1, NQ - 1)], y_rsem)
    wait_bytes(tan_ref.at[pl.ds(1, NQ - 1)], t_ssem)
    wait_bytes(asend, a_ssem)
    wait_bytes(bsend, b_ssem)
    wait_bytes(zb.at[:, pl.ds(1, NZ - 1)], z_ssem)
    wait_bytes(cot_ref.at[pl.ds(1, NQ - 1)], y_ssem)


def sums_kernel(
    cv_ref, dir_ref, res_ref, damp_ref, out_ref, sum_ref,
    first, second, mine, group, c_ssem, c_rsem, a_ssem, a_rsem, b_ssem, b_rsem,
):
    at = Place()
    depth = cv_ref.shape[2]
    ff = cv_ref.shape[1]
    step = 16
    near = [(dz, dc) for dz in range(NZ) for dc in range(NC)][1:]
    wide = [(dy, dx) for dy in range(NY) for dx in range(NX)][1:]
    zc = [(at.expert(0, dz, dc), at.x) for dz, dc in near]
    yx = [(at.expert(dy, 0, 0), at.xi(dx)) for dy, dx in wide]
    enter(zc + yx)
    for d in (2, 1, 3):
        send(cv_ref.at[at.xi(d)], out_ref.at[at.x], c_ssem, c_rsem.at[NX - d], at.dx(d))
    scale = 1.0 / damp_ref[0]
    totals = (jnp.zeros((8, 128), F32),) * 4
    for d in (0, 1, 3, 2):
        who = at.xi(d)
        if d:
            wait_bytes(out_ref.at[who], c_rsem.at[d])

        def part(i, sums, d=d, who=who):
            sub = pl.ds(pl.multiple_of(i * step, step), step)
            cols = pl.ds(pl.multiple_of(who * depth, depth), depth)
            if d:
                c = out_ref[who, sub, :]
            else:
                c = cv_ref[who, sub, :]
                out_ref[who, sub, :] = c
            p = dir_ref[sub, cols].astype(F32)
            r = res_ref[sub, cols].astype(F32)
            g = p + c.astype(F32) * scale

            def fold(v):
                v = v[0:8] + v[8:16]
                t = v[:, 0:128]
                for j in range(1, depth // 128):
                    t = t + v[:, j * 128 : (j + 1) * 128]
                return t

            return (
                sums[0] + fold(p * g), sums[1] + fold(r * r),
                sums[2] + fold(r * g), sums[3] + fold(g * g),
            )

        totals = lax.fori_loop(0, ff // step, part, totals)
    row = lax.broadcasted_iota(jnp.int32, (8, 128), 0)
    tile = jnp.zeros((8, 128), F32)
    for i in range(4):
        tile = jnp.where(row == i, jnp.sum(totals[i]), tile)
    mine[...] = tile
    spot = at.z * NC + at.c
    first[spot] = tile
    for n, peer in enumerate(zc):
        send(mine, first.at[spot], a_ssem, a_rsem, peer)
    wait_bytes(first.at[pl.ds(0, 15)], a_rsem)
    tile = first[0]
    for i in range(1, NZ * NC):
        tile = tile + first[i]
    group[...] = tile
    spot = at.y * NX + at.x
    second[spot] = tile
    for n, peer in enumerate(yx):
        send(group, second.at[spot], b_ssem, b_rsem, peer)
    wait_bytes(second.at[pl.ds(0, 15)], b_rsem)
    tile = second[0]
    for i in range(1, NY * NX):
        tile = tile + second[i]
    sum_ref[...] = tile
    wait_bytes(first.at[pl.ds(0, 15)], a_ssem)
    wait_bytes(second.at[pl.ds(0, 15)], b_ssem)
    wait_bytes(out_ref.at[pl.ds(0, 3)], c_ssem)


def final_kernel(damp_ref, sum_ref, cv_ref, dir_ref, res_ref, step_ref, newr_ref, newd_ref):
    scale = 1.0 / damp_ref[0]
    pq, rr = sum_ref[0:1, 0:1], sum_ref[1:2, 0:1]
    rq, qq = sum_ref[2:3, 0:1], sum_ref[3:4, 0:1]
    alpha = rr / pq
    beta = (rr - 2.0 * alpha * rq + alpha * alpha * qq) / rr
    p = dir_ref[...].astype(F32)
    g = p + cv_ref[0].astype(F32) * scale
    updated = res_ref[...].astype(F32) - alpha * g
    step_ref[...] = (alpha * p).astype(BF)
    newr_ref[...] = updated.astype(BF)
    newd_ref[...] = (updated + beta * p).astype(BF)


def params(ident):
    return pltpu.CompilerParams(collective_id=ident, has_side_effects=True)


def per_device(
    tokens, routes, route_gates, loss_weights, damping, w_gate, w_up, direction, residual
):
    dma = pltpu.SemaphoreType.DMA
    depth = tokens.shape[1]
    ff_loc, width = direction.shape[1:]
    ff = ff_loc * NX
    per_q = NZ * CAP
    search, resid = direction[0], residual[0]
    shape = jax.ShapeDtypeStruct

    arrived, weights, search_cols, table = pl.pallas_call(
        tokens_kernel,
        out_shape=(
            shape((NQ, per_q, depth), BF), shape((depth, 2 * ff), BF),
            shape((NX, ff_loc, depth), BF), shape((NZ, 2 * NQ, TOK), F32),
        ),
        in_specs=[VMEM, VMEM, VMEM, ANY, ANY, ANY],
        out_specs=(VMEM, VMEM, VMEM, VMEM),
        scratch_shapes=[
            pltpu.VMEM((NZ, 2 * NQ, TOK), F32), pltpu.VMEM((4, NQ * 2 * CAP, 2 * TOK), BF),
            pltpu.VMEM((NK, NZ, TOK, CH), BF), pltpu.VMEM((NQ, per_q, depth), BF),
            pltpu.VMEM((width, ff_loc), BF), pltpu.VMEM((width, ff_loc), BF),
            pltpu.VMEM((NX, depth, 2 * ff_loc), BF), pltpu.VMEM((NX, depth, 2 * ff_loc), BF),
            dma, dma((NZ,)), dma, dma((NK, NZ)), dma, dma, dma, dma, dma, dma, dma((3,)),
        ],
        compiler_params=params(0),
        name="tokens_kernel",
    )(routes.T, route_gates.T, tokens, w_gate[0], w_up[0], search)

    products = jnp.dot(
        arrived.reshape(NQ * per_q, depth), weights, preferred_element_type=F32
    ).astype(BF)
    group = NQ * per_q // NX
    subs = 4
    small = (subs, group // subs, 2 * ff)
    hidden = pl.pallas_call(
        hidden_kernel,
        out_shape=shape((NX, group, ff), BF),
        in_specs=[VMEM],
        out_specs=VMEM,
        scratch_shapes=[pltpu.VMEM(small, BF)] * 4
        + [dma, dma((subs,)), dma, dma((subs,)), dma, dma((subs,)), dma, dma((subs, 3))],
        compiler_params=params(1),
        name="hidden_kernel",
    )(products.reshape(NX, group, 2 * ff))
    hidden = hidden.reshape(NQ * per_q, ff)
    tangent = jnp.dot(
        hidden, search_cols.reshape(ff, depth), preferred_element_type=F32
    ).astype(BF)
    block = (TOK, CH)
    cotangent = pl.pallas_call(
        cotangent_kernel,
        out_shape=shape((NQ, per_q, depth), BF),
        in_specs=[VMEM, VMEM, VMEM],
        out_specs=VMEM,
        scratch_shapes=[
            pltpu.VMEM((4, 2 * TOK, NQ * 2 * CAP), BF), pltpu.VMEM((4, NQ * 2 * CAP, 2 * TOK), BF),
            pltpu.VMEM((NQ, per_q, depth), BF), pltpu.VMEM((NK,) + block, F32),
            pltpu.VMEM((NK, 4) + block, BF), pltpu.VMEM((NK, 4) + block, BF),
            pltpu.VMEM((NK, 3) + block, BF), pltpu.VMEM((NK, 3) + block, BF),
            pltpu.VMEM((NK, NZ) + block, BF), pltpu.VMEM((NQ, per_q, depth), BF),
            dma, dma((NK, 4)), dma, dma((NK, 4)), dma, dma((NK, 3)), dma, dma((NK, NZ)), dma, dma,
        ],
        compiler_params=params(2),
        name="cotangent_kernel",
    )(tangent.reshape(NQ, per_q, depth), table, loss_weights[:, None])
    curvature = lax.dot_general(
        hidden, cotangent.reshape(NQ * per_q, depth), (((0,), (0,)), ((), ())),
        preferred_element_type=F32,
    ).astype(BF)
    smem = pl.BlockSpec(memory_space=pltpu.SMEM)
    tile = (8, 128)
    mine, sums = pl.pallas_call(
        sums_kernel,
        out_shape=(shape((NX, ff_loc, depth), BF), shape(tile, F32)),
        in_specs=[VMEM, VMEM, VMEM, smem],
        out_specs=(VMEM, VMEM),
        scratch_shapes=[
            pltpu.VMEM((16,) + tile, F32), pltpu.VMEM((16,) + tile, F32),
            pltpu.VMEM(tile, F32), pltpu.VMEM(tile, F32),
            dma, dma((NX,)), dma, dma, dma, dma,
        ],
        compiler_params=params(3),
        name="sums_kernel",
    )(curvature.reshape(NX, ff_loc, depth), search, resid, damping)
    flat = pl.BlockSpec((ff_loc, depth), lambda i: (0, i))
    outs = pl.pallas_call(
        final_kernel,
        out_shape=(shape((ff_loc, width), BF),) * 3,
        grid=(NX,),
        in_specs=[
            smem, pl.BlockSpec(tile, lambda i: (0, 0)),
            pl.BlockSpec((1, ff_loc, depth), lambda i: (i, 0, 0)), flat, flat,
        ],
        out_specs=(flat, flat, flat),
        name="final_kernel",
    )(damping, sums, mine, search, resid)
    return tuple(o[None] for o in outs)


def solution(mesh):
    return jax.shard_map(
        per_device,
        mesh=mesh,
        in_specs=(
            P("expert", "hidden"),
            P("expert", None),
            P("expert", None),
            P("expert"),
            P(),
            P("expert", None, "hidden"),
            P("expert", None, "hidden"),
            P("expert", "hidden", None),
            P("expert", "hidden", None),
        ),
        out_specs=(
            P("expert", "hidden", None),
            P("expert", "hidden", None),
            P("expert", "hidden", None),
        ),
        check_vma=False,
    )
```

time: 836 us -> 284 us (0.34)
  blocking collectives: 555 us -> 0 us
  Pallas kernels: 0 us -> 255 us
  waiting for transfers between devices: 120 us -> 0 us
  local copies, waits for them, and re-layouts: 64.5 us -> 7.19 us
  other arithmetic: 44 us -> 0 us
  between operations: 17.6 us -> 1.35 us
  starting transfers between devices: 10.8 us -> 0 us
    all_to_all x3 -> x0, blocking collectives: 407 us -> none  [the longest x1 289 us: per_device(): lax.all_to_all(send_rows, 'expert', split_axis=0, concat_axis=0, tiled=True)]
    pallas_call x0 -> x5, Pallas kernels: none -> 255 us  [the longest x1 80.8 us: per_device(): pl.pallas_call(cotangent_kernel, out_shape=shape((NQ, per_q, depth), BF),...]
    psum x2 -> x0, blocking collectives: 148 us -> none  [the longest x1 74.3 us: per_device(): rr_new = lax.psum(jnp.sum(updated * updated), ('expert', 'hidden'))]
    all_to_all x2 -> x0, waiting for transfers between devices: 110 us -> none  [the longest x1 73 us: per_device(): lax.all_to_all(tangent.reshape(experts, capacity, -1), 'expert', split_ax...]
    gather x3 -> x0, local copies, waits for them, and re-layouts: 41.4 us -> none  [the longest x2 33 us: pack_rows(): picked = source_rows[index]]
    another operation x3 -> x0, other arithmetic: 18.2 us -> none
    div x3 -> x0, local copies, waits for them, and re-layouts: 11.4 us -> none  [per_device(): image = search + curvature / damping[0]]
    all_to_all x2 -> x0, starting transfers between devices: 10.7 us -> none  [the longest x1 6.04 us: per_device(): lax.all_to_all(tangent.reshape(experts, capacity, -1), 'expert', split_ax...]
  transfers between devices with their start and end apart: 4 -> 0, of which waited for: 4 -> 0; matrix products, arithmetic and copies ran while one was open for 3% -> 0% of each run, Pallas kernels for 0% -> 0%
where the time goes in v1:
time: 284 us
  Pallas kernels  255 us (90%)
  matrix products  20.5 us (7%)
  local copies, waits for them, and re-layouts  7.19 us (3%)
    pallas_call x1, Pallas kernels, per_device(): pl.pallas_call(cotangent_kernel, out_shape=shape((NQ, per_q, depth), BF),...  80.8 us
    pallas_call x1, Pallas kernels, per_device(): pl.pallas_call(tokens_kernel, out_shape=(shape((NQ, per_q, depth), BF), s...  68.3 us
    pallas_call x1, Pallas kernels, per_device(): pl.pallas_call(hidden_kernel, out_shape=shape((NX, group, ff), BF), in_sp...  63.7 us
    pallas_call x1, Pallas kernels, per_device(): pl.pallas_call(sums_kernel, out_shape=(shape((NX, ff_loc, depth), BF), sh...  35.9 us
    dot_general x1, matrix products, per_device(): jnp.dot(arrived.reshape(NQ * per_q, depth), weights, preferred_element_ty...  9.1 us
    unnamed x10, local copies, waits for them, and re-layouts  6.45 us
    pallas_call x1, Pallas kernels, per_device(): pl.pallas_call(final_kernel, out_shape=(shape((ff_loc, width), BF),) * 3,...  5.96 us
    dot_general x1, matrix products, per_device(): jnp.dot(hidden, search_cols.reshape(ff, depth), preferred_element_type=F32)  5.75 us

profile of v1, /device:TPU:1, one launch (start us, length us, event | category | flops | bytes accessed | tf_op | source)
XLA Modules:
  0.0 283.8 jit_solution(4971774887617318748)
XLA Ops:
  0.6 0.0 copy-start.1
  0.6 4.0 %copy.12 = bf16[1,4096,192]{2,1,0:T(8,128)(2,1)} copy(bf16[1,4096,192]{1,2,0:T(8,128)(2,1)} %param.14) | data formatting | bytes 3145728 | tf_op args[5]
  4.6 0.0 copy-done.1
  4.6 2.5 copy.13
  7.1 68.3 %tokens_kernel.1 = (bf16[8,192,1024]{2,1,0:T(8,128)(2,1)}, bf16[1024,1536]{1,0:T(8,128)(2,1)}, bf16[4,192,1024]{2,1,0:T(8,128)(2,1)}, f32[8,16,128]{2,1,0:T(8,128)}) custom-call(s32[8,128]{1,0:T(8,128)} %bitcast.36, f32[8,128]{1,0:T(8,128)} %bitcast.37, bf16[128,1024]{1,0:T(8,128)(2,1)} %tok_ref.1, bf16[4096,192]{1,0:T(8,128)(2,1)} %bitcast.26, ...), custom_call_target="tpu_custom_call" | custom-call | tf_op jit(solution)/shard_map/tokens_kernel/pallas_call | solution.py:514
  75.4 9.1 %convolution_convert_fusion = bf16[1536,1536]{1,0:T(8,128)(2,1)} fusion(bf16[1536,1024]{1,0:T(8,128)(2,1)} %bitcast.39, bf16[1024,1536]{1,0:T(8,128)(2,1)} %get-tuple-element.13), kind=kOutput, calls=%fused_computation | convolution fusion | flops 4834197504 | bytes 11010048 | tf_op jit(solution)/shard_map/dot_general | solution.py:533
  84.5 0.0 copy-start.3
  84.5 63.7 %hidden_kernel.1 = bf16[4,384,768]{2,1,0:T(8,128)(2,1)} custom-call(bf16[4,384,1536]{2,1,0:T(8,128)(2,1)} %bitcast.30), custom_call_target="tpu_custom_call" | custom-call | tf_op jit(solution)/shard_map/hidden_kernel/pallas_call | solution.py:539
  148.2 0.0 copy-done.3
  148.3 0.0 copy-start.2
  148.3 5.7 %convolution_convert_fusion.1 = bf16[1536,1024]{1,0:T(8,128)(2,1)} fusion(bf16[1536,768]{1,0:T(8,128)(2,1)} %bitcast.33, bf16[768,1024]{1,0:T(8,128)(2,1)S(1)} %bitcast.43), kind=kOutput, calls=%fused_computation.1 | convolution fusion | flops 2417491968 | bytes 7077888 | tf_op jit(solution)/shard_map/dot_general | solution.py:550
  154.0 0.0 copy-done.2
  154.0 0.7 copy.14.lw_ref
  154.8 0.0 copy-start
  154.8 80.8 %cotangent_kernel.1 = bf16[8,192,1024]{2,1,0:T(8,128)(2,1)} custom-call(bf16[8,192,1024]{2,1,0:T(8,128)(2,1)} %bitcast.31, f32[8,16,128]{2,1,0:T(8,128)} %get-tuple-element.15.tab_ref, f32[128,1]{1,0:T(8,128)} %copy.14.lw_ref), custom_call_target="tpu_custom_call" | custom-call | tf_op jit(solution)/shard_map/cotangent_kernel/pallas_call | solution.py:554
  235.6 0.0 copy-done
  235.6 5.6 %convolution_convert_fusion.2 = bf16[768,1024]{1,0:T(8,128)(2,1)} fusion(bf16[1536,768]{1,0:T(8,128)(2,1)S(1)} %bitcast.34, bf16[1536,1024]{1,0:T(8,128)(2,1)} %bitcast.32), kind=kOutput, calls=%fused_computation.2 | convolution fusion | flops 2416705536 | bytes 7077888 | tf_op jit(solution)/shard_map/dot_general | solution.py:570
  241.9 35.9 %sums_kernel.1 = (bf16[4,192,1024]{2,1,0:T(8,128)(2,1)}, f32[8,128]{1,0:T(8,128)}) custom-call(bf16[4,192,1024]{2,1,0:T(8,128)(2,1)} %bitcast.35, bf16[192,4096]{1,0:T(8,128)(2,1)} %bitcast.24, bf16[192,4096]{1,0:T(8,128)(2,1)} %bitcast.28, f32[1]{0:T(128)S(6)} %copy.15.damp_ref), custom_call_target="tpu_custom_call" | custom-call | tf_op jit(solution)/shard_map/sums_kernel/pallas_call | solution.py:576
  277.9 6.0 %final_kernel.1 = (bf16[192,4096]{1,0:T(8,128)(2,1)}, bf16[192,4096]{1,0:T(8,128)(2,1)}, bf16[192,4096]{1,0:T(8,128)(2,1)}) custom-call(f32[1]{0:T(128)S(6)} %copy.15.damp_ref, f32[8,128]{1,0:T(8,128)} %get-tuple-element.16.sum_ref, bf16[4,192,1024]{2,1,0:T(8,128)(2,1)} %get-tuple-element.17.cv_ref, bf16[192,4096]{1,0:T(8,128)(2,1)} %bitcast.25, ...), custom_call_target="tpu_custom_call" | custom-call | tf_op jit(solution)/shard_map/final_kernel/pallas_call | solution.py:590
Async XLA Ops:
  0.6 4.0 %copy-start.1 = (bf16[1,4096,192]{1,2,0:T(8,128)(2,1)S(1)}, bf16[1,4096,192]{1,2,0:T(8,128)(2,1)}, u32[]{:S(2)}) copy-start(bf16[1,4096,192]{1,2,0:T(8,128)(2,1)} %param.15) | copy-start | bytes 4718596
  84.5 63.8 %copy-start.3 = (bf16[4,192,1024]{2,1,0:T(8,128)(2,1)S(1)}, bf16[4,192,1024]{2,1,0:T(8,128)(2,1)}, u32[]{:S(2)}) copy-start(bf16[4,192,1024]{2,1,0:T(8,128)(2,1)} %get-tuple-element.14) | copy-start | bytes 4718596
  148.3 5.8 %copy-start.2 = (f32[128]{0:T(128)S(1)}, f32[128]{0:T(128)}, u32[]{:S(2)}) copy-start(f32[128]{0:T(128)} %param.12) | copy-start | bytes 1540
  154.8 80.9 %copy-start = (bf16[4,384,768]{2,1,0:T(8,128)(2,1)S(1)}, bf16[4,384,768]{2,1,0:T(8,128)(2,1)}, u32[]{:S(2)}) copy-start(bf16[4,384,768]{2,1,0:T(8,128)(2,1)} %hidden_kernel.1) | copy-start | bytes 7077892

commit v2 on v1

--- a/solution.py
+++ b/solution.py
@@ -38,6 +38,9 @@
 
     def dz(self, d):
         return (self.expert(0, d, 0), self.x)
+
+    def offset(self, dy, dz, dc, dx):
+        return (self.expert(dy, dz, dc), self.xi(dx))
 
     def dx(self, d):
         return (self.e, self.xi(d))
@@ -102,20 +105,22 @@
 def tokens_kernel(
     routes_ref, gates_ref, tok_ref, wg_ref, wu_ref, dir_ref,
     x_ref, w_ref, dirc_ref, tab_ref,
-    own_tab, slots, zb, ysend, wgv, wuv, wsend, wrecv,
+    own_tab, slots, zb, ysend,
     tab_ssem, tab_rsem, z_ssem, z_rsem, y_ssem, y_rsem, d_ssem, d_rsem, w_ssem, w_rsem, loc,
 ):
     at = Place()
-    wg_load = pltpu.make_async_copy(wg_ref, wgv, loc.at[0])
-    wu_load = pltpu.make_async_copy(wu_ref, wuv, loc.at[1])
-    wg_load.start()
-    wu_load.start()
     depth = dir_ref.shape[1] // NX
-    ff = dir_ref.shape[0]
-    own_dir = pltpu.make_async_copy(
-        dir_ref.at[:, pl.ds(pl.multiple_of(at.x * depth, depth), depth)], dirc_ref.at[at.x], loc.at[2]
-    )
-    own_dir.start()
+
+    def block(d, width=depth):
+        return pl.ds(pl.multiple_of(at.xi(d) * depth, depth), width)
+
+    own = [
+        pltpu.make_async_copy(wg_ref.at[:, block(0)], w_ref.at[0, at.x], loc.at[0]),
+        pltpu.make_async_copy(wu_ref.at[:, block(0)], w_ref.at[1, at.x], loc.at[1]),
+        pltpu.make_async_copy(dir_ref.at[:, block(0, CH)], dirc_ref.at[at.x], loc.at[2]),
+    ]
+    for copy in own:
+        copy.start()
 
     row = lax.broadcasted_iota(jnp.int32, (NZ * NQ, TOK), 0)
     ids = (
@@ -152,30 +157,10 @@
                 tok_ref.at[:, lanes(k)], zb.at[k, rel(-d)], z_ssem, z_rsem.at[k, rel(-d)], at.dz(d)
             )
     for d in (2, 1, 3):
-        send(
-            dir_ref.at[:, pl.ds(pl.multiple_of(at.xi(d) * depth, depth), depth)],
-            dirc_ref.at[at.x], d_ssem, d_rsem, at.dx(d),
-        )
-
-    wg_load.wait()
-    wu_load.wait()
-    step = 64
-    for d in (2, 1, 3, 0):
-        base = at.xi(d) * depth
-
-        def join(i, _, d=d, base=base):
-            rows = pl.ds(pl.multiple_of(base + i * step, step), step)
-            both = jnp.concatenate([wgv[rows, :], wuv[rows, :]], axis=1)
-            out_rows = pl.ds(pl.multiple_of(i * step, step), step)
-            if d == 0:
-                wrecv[at.x, out_rows, :] = both
-            else:
-                wsend[d, out_rows, :] = both
-            return 0
-
-        lax.fori_loop(0, depth // step, join, 0)
-        if d:
-            send(wsend.at[d], wrecv.at[at.x], w_ssem, w_rsem, at.dx(d))
+        send(wg_ref.at[:, block(d)], w_ref.at[0, at.x], w_ssem, w_rsem, at.dx(d))
+        send(wu_ref.at[:, block(d)], w_ref.at[1, at.x], w_ssem, w_rsem, at.dx(d))
+    for d in (2, 1, 3):
+        send(dir_ref.at[:, block(d, CH)], dirc_ref.at[at.x], d_ssem, d_rsem, at.dx(d))
 
     for s in range(1, 5):
         pi = s - 1
@@ -199,8 +184,8 @@
                 )
             r0, r1 = pair_blocks(pi)
             first = tok_ref[:, lanes(k)] if r0 == 0 else zb[k, r0]
-            block = jnp.concatenate([first, zb[k, r1]], axis=0)
-            picked = jnp.dot(slots[pi], block, preferred_element_type=F32).astype(BF)
+            both = jnp.concatenate([first, zb[k, r1]], axis=0)
+            picked = jnp.dot(slots[pi], both, preferred_element_type=F32).astype(BF)
             rows = pl.ds(pi * 2 * CAP, 2 * CAP)
             x_ref[0, rows, lanes(k)] = picked[0 : 2 * CAP]
             for q in range(1, NQ):
@@ -211,25 +196,16 @@
                     y_ssem, y_rsem, at.q(q),
                 )
 
-    own_dir.wait()
-    wait_bytes(wsend.at[pl.ds(1, 3)], w_rsem)
-
-    def split(i, _):
-        rows = pl.ds(pl.multiple_of(i * step, step), step)
-        parts = [wrecv[j, rows, :] for j in range(NX)]
-        w_ref[rows, :] = jnp.concatenate(
-            [p[:, :ff] for p in parts] + [p[:, ff:] for p in parts], axis=1
-        )
-        return 0
-
-    lax.fori_loop(0, depth // step, split, 0)
-    wait_bytes(dirc_ref.at[pl.ds(1, 3)], d_rsem)
-    wait_bytes(x_ref.at[pl.ds(1, NQ - 1)], y_rsem)
+    for copy in own:
+        copy.wait()
+    for sem in (w_rsem, w_ssem):
+        wait_bytes(w_ref.at[:, pl.ds(1, 3)], sem)
+    for sem in (d_rsem, d_ssem):
+        wait_bytes(dirc_ref.at[pl.ds(1, 3)], sem)
+    for sem in (y_rsem, y_ssem):
+        wait_bytes(x_ref.at[pl.ds(1, NQ - 1)], sem)
     wait_bytes(own_tab.at[pl.ds(1, NZ - 1)], tab_ssem)
     wait_bytes(zb.at[:, pl.ds(1, NZ - 1)], z_ssem)
-    wait_bytes(x_ref.at[pl.ds(1, NQ - 1)], y_ssem)
-    wait_bytes(dirc_ref.at[pl.ds(1, 3)], d_ssem)
-    wait_bytes(wsend.at[pl.ds(1, 3)], w_ssem)
 
 
 def hidden_kernel(
@@ -305,35 +281,59 @@
     wait_bytes(h_ref.at[pl.ds(0, 3)], h_ssem)
 
 
-def cotangent_kernel(
-    tan_ref, tab_ref, lw_ref, cot_ref,
-    back, fwd, recv, own, asend, arecv, bsend, brecv, zb, ysend,
-    t_ssem, t_rsem, a_ssem, a_rsem, b_ssem, b_rsem, z_ssem, z_rsem, y_ssem, y_rsem,
+GAP = 3
+
+
+def curvature_kernel(
+    damp_ref, hid_ref, first_ref, tab_ref, lw_ref, dir_ref, res_ref, out_ref, sum_ref,
+    back, fwd, turned, dcols, tsend, recv, own, asend, arecv, bsend, brecv, zb, ysend, cot, csend,
+    gather1, gather2, mine, group,
+    d_ssem, d_rsem, t_ssem, t_rsem, a_ssem, a_rsem, b_ssem, b_rsem, z_ssem, z_rsem,
+    y_ssem, y_rsem, c_ssem, c_rsem, r_ssem, r_rsem, s_ssem, s_rsem,
 ):
     at = Place()
-
-    def rows(pi):
-        return pl.ds(pi * 2 * CAP, 2 * CAP)
-
-    enter([at.q(q) for q in range(1, NQ)] + [at.dz(1), at.dz(-1)])
-    for t in range(NK + 3):
-        for k in range(NK):
-            if 0 <= t - k < 4:
-                pi = 3 - (t - k)
-                for q in range(1, NQ):
-                    send(
-                        tan_ref.at[q, rows(pi), lanes(k)], recv.at[inverse(q), rows(pi), lanes(k)],
-                        t_ssem, t_rsem.at[k, pi], at.q(q),
-                    )
-    for pi in (3, 2, 1, 0):
-        both = slot_matrix(tab_ref, pi, True)
-        fwd[pi] = both.astype(BF)
-        back[pi] = both.T.astype(BF)
+    ff, depth = dcols.shape[1] * NX, dcols.shape[2]
+    ff_loc = dcols.shape[1]
+    per_q = NZ * CAP
+    near = [(0, dz, dc, 0) for dz in range(NZ) for dc in range(NC)][1:]
+    wide = [(dy, 0, 0, dx) for dy in range(NY) for dx in range(NX)][1:]
+    diag = [(dy, 0, 1, 0) for dy in range(1, NY)]
+    enter([at.offset(*o) for o in near + wide + diag])
+
+    def rows(q, pi):
+        return pl.ds(q * per_q + pi * 2 * CAP, 2 * CAP)
+
+    rest = pl.ds(per_q, (NQ - 1) * per_q)
+
+    for k in range(1, NK):
+        for d in (2, 1, 3):
+            cols = pl.ds(pl.multiple_of(at.xi(d) * depth + k * CH, CH), CH)
+            send(
+                dir_ref.at[:, cols], dcols.at[at.x, :, lanes(k)], d_ssem, d_rsem.at[k], at.dx(d)
+            )
+
+    def tangent(k):
+        if k:
+            cols = pl.ds(pl.multiple_of(at.x * depth + k * CH, CH), CH)
+            dcols[at.x, :, lanes(k)] = dir_ref[:, cols]
+            wait_bytes(dcols.at[pl.ds(1, 3), :, lanes(k)], d_rsem.at[k])
+            search = dcols[:, :, lanes(k)].reshape(ff, CH)
+        else:
+            search = first_ref[...].reshape(ff, CH)
+        tsend[:, lanes(k)] = jnp.dot(
+            hid_ref[...], search, preferred_element_type=F32
+        ).astype(BF)
+        for pi in (3, 2, 1, 0):
+            for q in range(1, NQ):
+                send(
+                    tsend.at[rows(q, pi), lanes(k)], recv.at[rows(inverse(q), pi), lanes(k)],
+                    t_ssem, t_rsem.at[k, pi], at.q(q),
+                )
 
     def partial(k, pi):
-        wait_bytes(recv.at[pl.ds(1, NQ - 1), rows(pi), lanes(k)], t_rsem.at[k, pi])
+        wait_bytes(recv.at[pl.ds(0, (NQ - 1) * 2 * CAP), lanes(k)], t_rsem.at[k, pi])
         arrived = jnp.concatenate(
-            [tan_ref[0, rows(pi), lanes(k)]] + [recv[q, rows(pi), lanes(k)] for q in range(1, NQ)],
+            [tsend[rows(0, pi), lanes(k)]] + [recv[rows(q, pi), lanes(k)] for q in range(1, NQ)],
             axis=0,
         )
         return jnp.dot(back[pi], arrived, preferred_element_type=F32)
@@ -348,7 +348,6 @@
                 own[k] = low
                 asend[k, 0] = high.astype(BF)
             else:
-                s = 4 - n
                 ahead, behind = (low, high) if d == 1 else (high, low)
                 wait_bytes(arecv.at[k, n - 1], a_rsem.at[k, n - 1])
                 asend[k, n] = (arecv[k, n - 1].astype(F32) + ahead).astype(BF)
@@ -383,103 +382,111 @@
                 z_ssem, z_rsem.at[k, rel(d * (s + 1))], at.dz(-d),
             )
         r0, r1 = pair_blocks(pi)
-        block = jnp.concatenate([zb[k, r0], zb[k, r1]], axis=0)
-        picked = jnp.dot(fwd[pi], block, preferred_element_type=F32).astype(BF)
-        cot_ref[0, rows(pi), lanes(k)] = picked[0 : 2 * CAP]
+        both = jnp.concatenate([zb[k, r0], zb[k, r1]], axis=0)
+        picked = jnp.dot(fwd[pi], both, preferred_element_type=F32).astype(BF)
+        cot[rows(0, pi), lanes(k)] = picked[0 : 2 * CAP]
         for q in range(1, NQ):
-            ysend[q, rows(pi), lanes(k)] = picked[q * 2 * CAP : (q + 1) * 2 * CAP]
+            ysend[rows(q, pi), lanes(k)] = picked[q * 2 * CAP : (q + 1) * 2 * CAP]
         for q in range(1, NQ):
             send(
-                ysend.at[q, rows(pi), lanes(k)], cot_ref.at[inverse(q), rows(pi), lanes(k)],
-                y_ssem, y_rsem, at.q(q),
+                ysend.at[rows(q, pi), lanes(k)], cot.at[rows(inverse(q), pi), lanes(k)],
+                y_ssem, y_rsem.at[k], at.q(q),
             )
 
-    for t in range(NK + 8):
-        for k in range(NK):
-            if 0 <= t - k < 9:
-                stage(k, t - k)
-
-    wait_bytes(cot_ref.at[pl.ds(1, NQ - 1)], y_rsem)
-    wait_bytes(tan_ref.at[pl.ds(1, NQ - 1)], t_ssem)
+    def turn():
+        turned[...] = hid_ref[...].T
+
+    def matrices():
+        for pi in (3, 2, 1, 0):
+            both = slot_matrix(tab_ref, pi, True)
+            fwd[pi] = both.astype(BF)
+            back[pi] = both.T.astype(BF)
+
+    def curvature(k):
+        wait_bytes(cot.at[rest, lanes(k)], y_rsem.at[k])
+        csend[k] = jnp.dot(
+            turned[...], cot[:, lanes(k)], preferred_element_type=F32
+        ).astype(BF).reshape(NX, ff_loc, CH)
+        for d in (2, 1, 3):
+            send(csend.at[k, at.xi(d)], out_ref.at[at.x, :, lanes(k)], c_ssem, c_rsem.at[k], at.dx(d))
+        out_ref[at.x, :, lanes(k)] = csend[k, at.x]
+
+    scale = 1.0 / damp_ref[0]
+    step = 16
+
+    def total(k, sums):
+        wait_bytes(out_ref.at[pl.ds(1, 3), :, lanes(k)], c_rsem.at[k])
+
+        def part(i, sums):
+            sub = pl.ds(pl.multiple_of(i * step, step), step)
+            for j in range(NX):
+                cols = pl.ds(j * depth + k * CH, CH)
+                p = dir_ref[sub, cols].astype(F32)
+                r = res_ref[sub, cols].astype(F32)
+                g = p + out_ref[j, sub, lanes(k)].astype(F32) * scale
+
+                def fold(v):
+                    v = v[0:8] + v[8:16]
+                    return v[:, 0:128] + v[:, 128:256]
+
+                sums = (
+                    sums[0] + fold(p * g), sums[1] + fold(r * r),
+                    sums[2] + fold(r * g), sums[3] + fold(g * g),
+                )
+            return sums
+
+        return lax.fori_loop(0, ff_loc // step, part, sums)
+
+    tangent(0)
+    matrices()
+    events = [(GAP * k + n, 1, k, n) for k in range(NK) for n in range(9)]
+    events += [(GAP * k - 2, 0, k, 0) for k in range(1, NK)] + [(4, 2, 0, 0)]
+    for _, kind, k, n in sorted(events):
+        if kind == 0:
+            tangent(k)
+        elif kind == 1:
+            stage(k, n)
+        else:
+            turn()
+    for k in range(NK):
+        curvature(k)
+    sums = (jnp.zeros((8, 128), F32),) * 4
+    for k in range(NK):
+        sums = total(k, sums)
+
+    row = lax.broadcasted_iota(jnp.int32, (8, 128), 0)
+    tile = jnp.zeros((8, 128), F32)
+    for i in range(4):
+        tile = jnp.where(row == i, jnp.sum(sums[i]), tile)
+    mine[...] = tile
+    spot = at.z * NC + at.c
+    gather1[spot] = tile
+    for o in near:
+        send(mine, gather1.at[spot], r_ssem, r_rsem, at.offset(*o))
+    wait_bytes(gather1.at[pl.ds(0, 15)], r_rsem)
+    tile = gather1[0]
+    for i in range(1, NZ * NC):
+        tile = tile + gather1[i]
+    group[...] = tile
+    spot = at.y * NX + at.x
+    gather2[spot] = tile
+    for o in wide:
+        send(group, gather2.at[spot], s_ssem, s_rsem, at.offset(*o))
+    wait_bytes(gather2.at[pl.ds(0, 15)], s_rsem)
+    tile = gather2[0]
+    for i in range(1, NY * NX):
+        tile = tile + gather2[i]
+    sum_ref[...] = tile
+
+    wait_bytes(dcols.at[pl.ds(1, 3), :, pl.ds(CH, (NK - 1) * CH)], d_ssem)
+    wait_bytes(tsend.at[rest], t_ssem)
     wait_bytes(asend, a_ssem)
     wait_bytes(bsend, b_ssem)
     wait_bytes(zb.at[:, pl.ds(1, NZ - 1)], z_ssem)
-    wait_bytes(cot_ref.at[pl.ds(1, NQ - 1)], y_ssem)
-
-
-def sums_kernel(
-    cv_ref, dir_ref, res_ref, damp_ref, out_ref, sum_ref,
-    first, second, mine, group, c_ssem, c_rsem, a_ssem, a_rsem, b_ssem, b_rsem,
-):
-    at = Place()
-    depth = cv_ref.shape[2]
-    ff = cv_ref.shape[1]
-    step = 16
-    near = [(dz, dc) for dz in range(NZ) for dc in range(NC)][1:]
-    wide = [(dy, dx) for dy in range(NY) for dx in range(NX)][1:]
-    zc = [(at.expert(0, dz, dc), at.x) for dz, dc in near]
-    yx = [(at.expert(dy, 0, 0), at.xi(dx)) for dy, dx in wide]
-    enter(zc + yx)
-    for d in (2, 1, 3):
-        send(cv_ref.at[at.xi(d)], out_ref.at[at.x], c_ssem, c_rsem.at[NX - d], at.dx(d))
-    scale = 1.0 / damp_ref[0]
-    totals = (jnp.zeros((8, 128), F32),) * 4
-    for d in (0, 1, 3, 2):
-        who = at.xi(d)
-        if d:
-            wait_bytes(out_ref.at[who], c_rsem.at[d])
-
-        def part(i, sums, d=d, who=who):
-            sub = pl.ds(pl.multiple_of(i * step, step), step)
-            cols = pl.ds(pl.multiple_of(who * depth, depth), depth)
-            if d:
-                c = out_ref[who, sub, :]
-            else:
-                c = cv_ref[who, sub, :]
-                out_ref[who, sub, :] = c
-            p = dir_ref[sub, cols].astype(F32)
-            r = res_ref[sub, cols].astype(F32)
-            g = p + c.astype(F32) * scale
-
-            def fold(v):
-                v = v[0:8] + v[8:16]
-                t = v[:, 0:128]
-                for j in range(1, depth // 128):
-                    t = t + v[:, j * 128 : (j + 1) * 128]
-                return t
-
-            return (
-                sums[0] + fold(p * g), sums[1] + fold(r * r),
-                sums[2] + fold(r * g), sums[3] + fold(g * g),
-            )
-
-        totals = lax.fori_loop(0, ff // step, part, totals)
-    row = lax.broadcasted_iota(jnp.int32, (8, 128), 0)
-    tile = jnp.zeros((8, 128), F32)
-    for i in range(4):
-        tile = jnp.where(row == i, jnp.sum(totals[i]), tile)
-    mine[...] = tile
-    spot = at.z * NC + at.c
-    first[spot] = tile
-    for n, peer in enumerate(zc):
-        send(mine, first.at[spot], a_ssem, a_rsem, peer)
-    wait_bytes(first.at[pl.ds(0, 15)], a_rsem)
-    tile = first[0]
-    for i in range(1, NZ * NC):
-        tile = tile + first[i]
-    group[...] = tile
-    spot = at.y * NX + at.x
-    second[spot] = tile
-    for n, peer in enumerate(yx):
-        send(group, second.at[spot], b_ssem, b_rsem, peer)
-    wait_bytes(second.at[pl.ds(0, 15)], b_rsem)
-    tile = second[0]
-    for i in range(1, NY * NX):
-        tile = tile + second[i]
-    sum_ref[...] = tile
-    wait_bytes(first.at[pl.ds(0, 15)], a_ssem)
-    wait_bytes(second.at[pl.ds(0, 15)], b_ssem)
-    wait_bytes(out_ref.at[pl.ds(0, 3)], c_ssem)
+    wait_bytes(cot.at[rest], y_ssem)
+    wait_bytes(csend.at[:, pl.ds(1, 3)], c_ssem)
+    wait_bytes(gather1.at[pl.ds(0, 15)], r_ssem)
+    wait_bytes(gather2.at[pl.ds(0, 15)], s_ssem)
 
 
 def final_kernel(damp_ref, sum_ref, cv_ref, dir_ref, res_ref, step_ref, newr_ref, newd_ref):
@@ -511,29 +518,29 @@
     search, resid = direction[0], residual[0]
     shape = jax.ShapeDtypeStruct
 
-    arrived, weights, search_cols, table = pl.pallas_call(
+    slots = NQ * per_q
+    arrived, weights, first_cols, table = pl.pallas_call(
         tokens_kernel,
         out_shape=(
-            shape((NQ, per_q, depth), BF), shape((depth, 2 * ff), BF),
-            shape((NX, ff_loc, depth), BF), shape((NZ, 2 * NQ, TOK), F32),
+            shape((NQ, per_q, depth), BF), shape((2, NX, ff_loc, depth), BF),
+            shape((NX, ff_loc, CH), BF), shape((NZ, 2 * NQ, TOK), F32),
         ),
         in_specs=[VMEM, VMEM, VMEM, ANY, ANY, ANY],
         out_specs=(VMEM, VMEM, VMEM, VMEM),
         scratch_shapes=[
             pltpu.VMEM((NZ, 2 * NQ, TOK), F32), pltpu.VMEM((4, NQ * 2 * CAP, 2 * TOK), BF),
             pltpu.VMEM((NK, NZ, TOK, CH), BF), pltpu.VMEM((NQ, per_q, depth), BF),
-            pltpu.VMEM((width, ff_loc), BF), pltpu.VMEM((width, ff_loc), BF),
-            pltpu.VMEM((NX, depth, 2 * ff_loc), BF), pltpu.VMEM((NX, depth, 2 * ff_loc), BF),
             dma, dma((NZ,)), dma, dma((NK, NZ)), dma, dma, dma, dma, dma, dma, dma((3,)),
         ],
         compiler_params=params(0),
         name="tokens_kernel",
-    )(routes.T, route_gates.T, tokens, w_gate[0], w_up[0], search)
-
-    products = jnp.dot(
-        arrived.reshape(NQ * per_q, depth), weights, preferred_element_type=F32
+    )(routes.T, route_gates.T, tokens, w_gate[0].T, w_up[0].T, search)
+
+    products = lax.dot_general(
+        arrived.reshape(slots, depth), weights.reshape(2 * ff, depth), (((1,), (1,)), ((), ())),
+        preferred_element_type=F32,
     ).astype(BF)
-    group = NQ * per_q // NX
+    group = slots // NX
     subs = 4
     small = (subs, group // subs, 2 * ff)
     hidden = pl.pallas_call(
@@ -546,46 +553,30 @@
         compiler_params=params(1),
         name="hidden_kernel",
     )(products.reshape(NX, group, 2 * ff))
-    hidden = hidden.reshape(NQ * per_q, ff)
-    tangent = jnp.dot(
-        hidden, search_cols.reshape(ff, depth), preferred_element_type=F32
-    ).astype(BF)
     block = (TOK, CH)
-    cotangent = pl.pallas_call(
-        cotangent_kernel,
-        out_shape=shape((NQ, per_q, depth), BF),
-        in_specs=[VMEM, VMEM, VMEM],
-        out_specs=VMEM,
+    tile = (8, 128)
+    smem = pl.BlockSpec(memory_space=pltpu.SMEM)
+    vmem = pltpu.VMEM
+    mine, sums = pl.pallas_call(
+        curvature_kernel,
+        out_shape=(shape((NX, ff_loc, depth), BF), shape(tile, F32)),
+        in_specs=[smem] + [VMEM] * 6,
+        out_specs=(VMEM, VMEM),
         scratch_shapes=[
-            pltpu.VMEM((4, 2 * TOK, NQ * 2 * CAP), BF), pltpu.VMEM((4, NQ * 2 * CAP, 2 * TOK), BF),
-            pltpu.VMEM((NQ, per_q, depth), BF), pltpu.VMEM((NK,) + block, F32),
-            pltpu.VMEM((NK, 4) + block, BF), pltpu.VMEM((NK, 4) + block, BF),
-            pltpu.VMEM((NK, 3) + block, BF), pltpu.VMEM((NK, 3) + block, BF),
-            pltpu.VMEM((NK, NZ) + block, BF), pltpu.VMEM((NQ, per_q, depth), BF),
-            dma, dma((NK, 4)), dma, dma((NK, 4)), dma, dma((NK, 3)), dma, dma((NK, NZ)), dma, dma,
+            vmem((4, 2 * TOK, NQ * 2 * CAP), BF), vmem((4, NQ * 2 * CAP, 2 * TOK), BF),
+            vmem((ff, slots), BF), vmem((NX, ff_loc, depth), BF),
+            vmem((slots, depth), BF), vmem((slots, depth), BF), vmem((NK,) + block, F32),
+            vmem((NK, 4) + block, BF), vmem((NK, 4) + block, BF),
+            vmem((NK, 3) + block, BF), vmem((NK, 3) + block, BF),
+            vmem((NK, NZ) + block, BF), vmem((slots, depth), BF), vmem((slots, depth), BF),
+            vmem((NK, NX, ff_loc, CH), BF),
+            vmem((16,) + tile, F32), vmem((16,) + tile, F32), vmem(tile, F32), vmem(tile, F32),
+            dma, dma((NK,)), dma, dma((NK, 4)), dma, dma((NK, 4)), dma, dma((NK, 3)),
+            dma, dma((NK, NZ)), dma, dma((NK,)), dma, dma((NK,)), dma, dma, dma, dma,
         ],
         compiler_params=params(2),
-        name="cotangent_kernel",
-    )(tangent.reshape(NQ, per_q, depth), table, loss_weights[:, None])
-    curvature = lax.dot_general(
-        hidden, cotangent.reshape(NQ * per_q, depth), (((0,), (0,)), ((), ())),
-        preferred_element_type=F32,
-    ).astype(BF)
-    smem = pl.BlockSpec(memory_space=pltpu.SMEM)
-    tile = (8, 128)
-    mine, sums = pl.pallas_call(
-        sums_kernel,
-        out_shape=(shape((NX, ff_loc, depth), BF), shape(tile, F32)),
-        in_specs=[VMEM, VMEM, VMEM, smem],
-        out_specs=(VMEM, VMEM),
-        scratch_shapes=[
-            pltpu.VMEM((16,) + tile, F32), pltpu.VMEM((16,) + tile, F32),
-            pltpu.VMEM(tile, F32), pltpu.VMEM(tile, F32),
-            dma, dma((NX,)), dma, dma, dma, dma,
-        ],
-        compiler_params=params(3),
-        name="sums_kernel",
-    )(curvature.reshape(NX, ff_loc, depth), search, resid, damping)
+        name="curvature_kernel",
+    )(damping, hidden.reshape(slots, ff), first_cols, table, loss_weights[:, None], search, resid)
     flat = pl.BlockSpec((ff_loc, depth), lambda i: (0, i))
     outs = pl.pallas_call(
         final_kernel,

time: 284 us -> 251 us (0.88)
  Pallas kernels: 255 us -> 239 us
  matrix products: 20.5 us -> 9.19 us
  local copies, waits for them, and re-layouts: 7.19 us -> 0.75 us
    pallas_call x1, Pallas kernels: 68.3 us -> 55.1 us  [per_device(): pl.pallas_call(tokens_kernel, out_shape=(shape((NQ, per_q, depth), BF), s...]
    dot_general x3 -> x1, matrix products: 20.5 us -> 9.19 us  [per_device(): lax.dot_general(arrived.reshape(slots, depth), weights.reshape(2 * ff, de...]
    unnamed x10 -> x2, local copies, waits for them, and re-layouts: 6.45 us -> 0.01 us
    pallas_call x2 -> x1, Pallas kernels: 117 us -> 114 us  [per_device(): pl.pallas_call(curvature_kernel, out_shape=(shape((NX, ff_loc, depth), BF...]
where the time goes in v2:
time: 251 us
  Pallas kernels  239 us (95%)
  matrix products  9.19 us (4%)
    pallas_call x1, Pallas kernels, per_device(): pl.pallas_call(curvature_kernel, out_shape=(shape((NX, ff_loc, depth), BF...  114 us
    pallas_call x1, Pallas kernels, per_device(): pl.pallas_call(hidden_kernel, out_shape=shape((NX, group, ff), BF), in_sp...  64 us
    pallas_call x1, Pallas kernels, per_device(): pl.pallas_call(tokens_kernel, out_shape=(shape((NQ, per_q, depth), BF), s...  55.1 us
    dot_general x1, matrix products, per_device(): lax.dot_general(arrived.reshape(slots, depth), weights.reshape(2 * ff, de...  9.19 us
    pallas_call x1, Pallas kernels, per_device(): pl.pallas_call(final_kernel, out_shape=(shape((ff_loc, width), BF),) * 3,...  5.9 us

profile of v2, /device:TPU:1, one launch (start us, length us, event | category | flops | bytes accessed | tf_op | source)
XLA Modules:
  0.0 250.7 jit_solution(6697959738652782716)
XLA Ops:
  0.6 55.1 %tokens_kernel.1 = (bf16[8,192,1024]{2,1,0:T(8,128)(2,1)}, bf16[2,4,192,1024]{3,2,1,0:T(8,128)(2,1)}, bf16[4,192,256]{2,1,0:T(8,128)(2,1)}, f32[8,16,128]{2,1,0:T(8,128)}) custom-call(s32[8,128]{1,0:T(8,128)} %bitcast.29, f32[8,128]{1,0:T(8,128)} %bitcast.30, bf16[128,1024]{1,0:T(8,128)(2,1)} %tok_ref.1, bf16[192,4096]{1,0:T(8,128)(2,1)} %bitcast.27, ...), custom_call_target="tpu_custom_call" | custom-call | tf_op jit(solution)/shard_map/tokens_kernel/pallas_call | solution.py:522
  55.8 9.2 %convolution_convert_fusion = bf16[1536,1536]{1,0:T(8,128)(2,1)} fusion(bf16[1536,1024]{1,0:T(8,128)(2,1)} %bitcast.32, bf16[1536,1024]{1,0:T(8,128)(2,1)} %bitcast.33), kind=kOutput, calls=%fused_computation | convolution fusion | flops 4834197504 | bytes 11010048 | tf_op jit(solution)/shard_map/dot_general | solution.py:539
  64.9 0.0 copy-start
  64.9 64.0 %hidden_kernel.1 = bf16[4,384,768]{2,1,0:T(8,128)(2,1)} custom-call(bf16[4,384,1536]{2,1,0:T(8,128)(2,1)} %bitcast.26), custom_call_target="tpu_custom_call" | custom-call | tf_op jit(solution)/shard_map/hidden_kernel/pallas_call | solution.py:546
  129.6 0.0 copy-done
  129.6 0.7 copy.12.lw_ref
  130.3 114.4 %curvature_kernel.1 = (bf16[4,192,1024]{2,1,0:T(8,128)(2,1)}, f32[8,128]{1,0:T(8,128)}) custom-call(f32[1]{0:T(128)S(6)} %copy.13.damp_ref, bf16[1536,768]{1,0:T(8,128)(2,1)} %bitcast.23, bf16[4,192,256]{2,1,0:T(8,128)(2,1)} %get-tuple-element.14.first_ref, f32[8,16,128]{2,1,0:T(8,128)} %get-tuple-element.15.tab_ref, f32[128,1]{1,0:T(8,128)} %copy.12.lw_ref, ...), custom_call_target="tpu_custom_call" | custom-call | tf_op jit(solution)/shard_map/curvature_kernel/pallas_call | solution.py:560
  244.8 5.9 %final_kernel.1 = (bf16[192,4096]{1,0:T(8,128)(2,1)}, bf16[192,4096]{1,0:T(8,128)(2,1)}, bf16[192,4096]{1,0:T(8,128)(2,1)}) custom-call(f32[1]{0:T(128)S(6)} %copy.13.damp_ref, f32[8,128]{1,0:T(8,128)} %get-tuple-element.16.sum_ref, bf16[4,192,1024]{2,1,0:T(8,128)(2,1)} %get-tuple-element.17.cv_ref, bf16[192,4096]{1,0:T(8,128)(2,1)} %bitcast.22, ...), custom_call_target="tpu_custom_call" | custom-call | tf_op jit(solution)/shard_map/final_kernel/pallas_call | solution.py:581
Async XLA Ops:
  64.9 64.7 %copy-start = (f32[128]{0:T(128)S(1)}, f32[128]{0:T(128)}, u32[]{:S(2)}) copy-start(f32[128]{0:T(128)} %param.12) | copy-start | bytes 1540
